TPU v7x, 512 devices: a whole 4x8x8 slice. The times are simulated.
512 devices in a mesh: tm: 32 (over z, x), frac: 16 (over y, core).
Axes of the slice: x: 4, y: 8, z: 8, core: 2. Of those that a mesh axis runs over, the one named last changes fastest.
Arguments:
- pressure0: float32 [64, 32, 128], P('frac'), may hold values from -6 to 6
- storage: float32 [64, 32, 128], P('frac'), may hold values from 0.1 to 1
- perm_base: float32 [64, 32, 128], P('frac'), may hold values from 0.2 to 5
- leakoff: float32 [64, 32, 128], P('frac'), may hold values from 0.5 to 2
- sources: float32 [32, 64, 32, 128], P('tm', 'frac'), may hold values from -6 to 6
- export_cells: int32 [4096], P('frac'), may hold values from 0 to 16383
- inter_local: int32 [16384], P('frac'), may hold values from 0 to 16383
- trace_source: int32 [16384], P('frac'), may hold values from 0 to 4095, as said below
- inter_trans: float32 [16384], P('frac'), may hold values from 0.5 to 4
- inter_count: int32 [16], P('frac'), may hold values from 1 to 1024, 8192 in all
Outputs:
- slice_pressure: float32 [32, 64, 32, 128], P('tm', 'frac')
Inputs may be any that keep to these rules, and one draw needn't show every extreme that they name: An entry of frac index d names a slot of another frac index: trace_source // 256 differs from d. `inter_count`: the live entries of a frac index are its first ones; the largest count is 1024.
All inputs are finite; a program needn't handle non-finite values. No bound on the sum of `inter_count` on one device may be relied on, other than what follows from the above.
Results may differ from a plain program's by a relative error of at most 0.00002.
Values sent between devices are 32-bit elements; how exact they have to be, the bound alone decides.
A program may use at most 64 MiB of HBM per device.

v0:
```python
import jax
import jax.numpy as jnp
from jax import lax
from jax.sharding import PartitionSpec as P

FINE_STEPS = 4
SWEEPS = 8
COARSE_SWEEPS = 2
ITERS = 2
stress_factor = 0.15
fine_size = 0.25


def next_rows(array):
    return jnp.concatenate([array[:, 1:, :], jnp.zeros_like(array[:, :1, :])], axis=1)


def prev_rows(array):
    return jnp.concatenate([jnp.zeros_like(array[:, :1, :]), array[:, :-1, :]], axis=1)


def next_cols(array):
    return jnp.concatenate([array[:, :, 1:], jnp.zeros_like(array[:, :, :1])], axis=2)


def prev_cols(array):
    return jnp.concatenate([jnp.zeros_like(array[:, :, :1]), array[:, :, :-1]], axis=2)


def implicit(pressure, slice_source, step_size, sweeps, fields, couple):
    storage, perm_base, leakoff, tisum = fields
    permeability = perm_base * jnp.exp(stress_factor * pressure)
    row_index = lax.broadcasted_iota(jnp.int32, pressure.shape, 1)
    col_index = lax.broadcasted_iota(jnp.int32, pressure.shape, 2)
    face_rows = jnp.where(
        row_index < pressure.shape[1] - 1, 0.5 * (permeability + next_rows(permeability)), 0.0
    )
    face_cols = jnp.where(
        col_index < pressure.shape[2] - 1, 0.5 * (permeability + next_cols(permeability)), 0.0
    )
    storage_rate = storage / step_size
    diagonal_total = (
        storage_rate + leakoff + face_rows + prev_rows(face_rows) + face_cols + prev_cols(face_cols)
    )
    right_side = storage_rate * pressure + slice_source
    if couple is not None:
        diagonal_total = diagonal_total + tisum
        right_side = right_side + couple(pressure)

    def sweep(sweep_index, current):
        beside = face_rows * next_rows(current) + prev_rows(face_rows * current)
        beside = beside + face_cols * next_cols(current) + prev_cols(face_cols * current)
        return (right_side + beside) / diagonal_total

    return lax.fori_loop(0, sweeps, sweep, pressure)


def body(
    pressure0,
    storage,
    perm_base,
    leakoff,
    sources,
    export_cells,
    inter_local,
    trace_source,
    inter_trans,
    inter_count,
):
    slice_count = lax.axis_size("tm")
    slice_index = lax.axis_index("tm")
    own_source = sources[0]
    entry_index = lax.broadcasted_iota(jnp.int32, inter_local.shape, 0)
    weights = jnp.where(entry_index < inter_count[0], inter_trans, jnp.zeros_like(inter_trans))
    cell_total = pressure0.size
    tisum = (
        jnp.zeros((cell_total,), jnp.float32).at[inter_local].add(weights).reshape(pressure0.shape)
    )
    fields = (storage, perm_base, leakoff, tisum)

    def couple(current):
        flat_field = current.reshape(-1)
        exported = flat_field[export_cells]
        gathered = lax.all_gather(exported, "frac", axis=0, tiled=True)
        remote_values = gathered[trace_source]
        return (
            jnp.zeros_like(flat_field)
            .at[inter_local]
            .add(weights * remote_values)
            .reshape(current.shape)
        )

    def coarse(pressure, slice_source):
        return implicit(pressure, slice_source, fine_size * FINE_STEPS, COARSE_SWEEPS, fields, None)

    all_sources = lax.all_gather(sources, "tm", axis=0, tiled=True)

    def chain(correction, carry_zero):
        if carry_zero:
            all_corrections = jnp.zeros_like(all_sources)
        else:
            all_corrections = lax.all_gather(correction[None], "tm", axis=0, tiled=True)

        def turn(turn_index, carried):
            current, kept_state = carried
            slice_source = lax.dynamic_index_in_dim(all_sources, turn_index, 0, keepdims=False)
            added = lax.dynamic_index_in_dim(all_corrections, turn_index, 0, keepdims=False)
            current = coarse(current, slice_source) + added
            kept_state = jnp.where(slice_index == turn_index + 1, current, kept_state)
            return (current, kept_state)

        final_pair = lax.fori_loop(0, slice_count - 1, turn, (pressure0, pressure0))
        return final_pair[1]

    state = chain(jnp.zeros_like(pressure0), True)
    for iteration in range(ITERS):
        fine_pressure = state
        for step_number in range(FINE_STEPS):
            fine_pressure = implicit(fine_pressure, own_source, fine_size, SWEEPS, fields, couple)
        coarse_end = coarse(state, own_source)
        state = chain(fine_pressure - coarse_end, False)
    return state[None]


def solution(mesh):
    placed = (
        P("frac", None, None),
        P("frac", None, None),
        P("frac", None, None),
        P("frac", None, None),
        P("tm", "frac", None, None),
        P("frac"),
        P("frac"),
        P("frac"),
        P("frac"),
        P("frac"),
    )
    return jax.shard_map(
        body, mesh=mesh, in_specs=placed, out_specs=P("tm", "frac", None, None), check_vma=False
    )
```

profile of v0, /device:TPU:8, one launch (start us, length us, event | category | flops | bytes accessed | tf_op | source)
XLA Modules:
  0.0 733.0 jit_solution(9327614761849319025)
XLA Ops:
  11.1 88.0 %all-gather.22.cloned.1.call-done = f32[32,4,32,128]{3,2,1,0:T(8,128)} async-done(((f32[1,4,32,128]{3,2,1,0:T(8,128)}), f32[32,4,32,128]{3,2,1,0:T(8,128)}) %all-gather.22.cloned.1.call-update) | async-done | bytes 2097168 | tf_op jit(solution)/shard_map/all_gather | solution.py:96
  99.1 52.9 %while.235 = (s32[]{:T(128)}, f32[4,32,128]{2,1,0:T(8,128)S(1)}, f32[4,32,128]{2,1,0:T(8,128)S(1)}, f32[4,32,128]{2,1,0:T(8,128)}, f32[4,32,128]{2,1,0:T(8,128)}...) while((s32[]{:T(128)}, f32[4,32,128]{2,1,0:T(8,128)S(1)}, ...), condition=%wide.region_3.4_spmd, body=%wide.region_0.3_spmd.sunk | while | flops 392741 | bytes 2790472 | solution.py:112
  154.8 15.7 %all-gather.10 = f32[16,1,256]{2,1,0:T(1,128)S(1)} all-gather(f32[1,1,256]{2,1,0:T(1,128)S(1)} %bitcast.174), channel_id=2, replica_groups=mesh['tm'=32,'frac'=16] {'frac'}, dimensions={0}, use_global_device_ids=true | all-gather | bytes 17408 | tf_op jit(solution)/shard_map/all_gather | solution.py:84
  170.5 6.1 gather_fusion.1
  182.6 5.9 scatter_custom_fusion
  192.2 16.0 %all-gather.11 = f32[16,1,256]{2,1,0:T(1,128)S(1)} all-gather(f32[1,1,256]{2,1,0:T(1,128)S(1)} %bitcast.175), channel_id=3, replica_groups=mesh['tm'=32,'frac'=16] {'frac'}, dimensions={0}, use_global_device_ids=true | all-gather | bytes 17408 | tf_op jit(solution)/shard_map/all_gather | solution.py:84
  208.2 6.1 gather_fusion.3
  224.1 15.2 %all-gather.12 = f32[16,1,256]{2,1,0:T(1,128)S(1)} all-gather(f32[1,1,256]{2,1,0:T(1,128)S(1)} %bitcast.176), channel_id=4, replica_groups=mesh['tm'=32,'frac'=16] {'frac'}, dimensions={0}, use_global_device_ids=true | all-gather | bytes 17408 | tf_op jit(solution)/shard_map/all_gather | solution.py:84
  239.3 6.1 gather_fusion.5
  245.5 5.9 scatter_custom_fusion.3
  255.2 15.1 %all-gather.13 = f32[16,1,256]{2,1,0:T(1,128)S(1)} all-gather(f32[1,1,256]{2,1,0:T(1,128)S(1)} %bitcast.177), channel_id=5, replica_groups=mesh['tm'=32,'frac'=16] {'frac'}, dimensions={0}, use_global_device_ids=true | all-gather | bytes 17408 | tf_op jit(solution)/shard_map/all_gather | solution.py:84
  270.3 6.1 gather_fusion.7
  285.8 79.1 %all-gather.24.cloned.1.call-done = f32[128,32,128]{2,1,0:T(8,128)} async-done(((f32[4,32,128]{2,1,0:T(8,128)}), f32[128,32,128]{2,1,0:T(8,128)}) %all-gather.24.cloned.1.call-update) | async-done | bytes 2097168 | tf_op jit(solution)/shard_map/all_gather | solution.py:102
  364.9 77.4 %while.242 = (s32[]{:T(128)}, f32[4,32,128]{2,1,0:T(8,128)S(1)}, f32[4,32,128]{2,1,0:T(8,128)S(1)}, f32[4,32,128]{2,1,0:T(8,128)S(1)}, f32[4,32,128]{2,1,0:T(8,1...) while((s32[]{:T(128)}, f32[4,32,128]{2,1,0:T(8,128)S(1)}, ...), condition=%wide.region_22.23_spmd, body=%wide.region_19.22_spmd.sunk | while | flops 409125 | bytes 2921564 | solution.py:112
  444.1 15.7 %all-gather.14 = f32[16,1,256]{2,1,0:T(1,128)S(1)} all-gather(f32[1,1,256]{2,1,0:T(1,128)S(1)} %bitcast.178), channel_id=7, replica_groups=mesh['tm'=32,'frac'=16] {'frac'}, dimensions={0}, use_global_device_ids=true | all-gather | bytes 17408 | tf_op jit(solution)/shard_map/all_gather | solution.py:84
  459.8 6.1 gather_fusion.9
  475.7 16.0 %all-gather.15 = f32[16,1,256]{2,1,0:T(1,128)S(1)} all-gather(f32[1,1,256]{2,1,0:T(1,128)S(1)} %bitcast.179), channel_id=8, replica_groups=mesh['tm'=32,'frac'=16] {'frac'}, dimensions={0}, use_global_device_ids=true | all-gather | bytes 17408 | tf_op jit(solution)/shard_map/all_gather | solution.py:84
  491.7 6.1 gather_fusion.11
  507.6 15.2 %all-gather.16 = f32[16,1,256]{2,1,0:T(1,128)S(1)} all-gather(f32[1,1,256]{2,1,0:T(1,128)S(1)} %bitcast.180), channel_id=9, replica_groups=mesh['tm'=32,'frac'=16] {'frac'}, dimensions={0}, use_global_device_ids=true | all-gather | bytes 17408 | tf_op jit(solution)/shard_map/all_gather | solution.py:84
  522.8 6.1 gather_fusion.13
  538.7 15.1 %all-gather.17 = f32[16,1,256]{2,1,0:T(1,128)S(1)} all-gather(f32[1,1,256]{2,1,0:T(1,128)S(1)} %bitcast.173), channel_id=10, replica_groups=mesh['tm'=32,'frac'=16] {'frac'}, dimensions={0}, use_global_device_ids=true | all-gather | bytes 17408 | tf_op jit(solution)/shard_map/all_gather | solution.py:84
  553.8 6.1 gather_fusion.15
  569.0 79.4 %all-gather.26.cloned.1.call-done = f32[128,32,128]{2,1,0:T(8,128)} async-done(((f32[4,32,128]{2,1,0:T(8,128)}), f32[128,32,128]{2,1,0:T(8,128)}) %all-gather.26.cloned.1.call-update) | async-done | bytes 2097168 | tf_op jit(solution)/shard_map/all_gather | solution.py:102
  648.4 77.4 %while.249 = (s32[]{:T(128)}, f32[4,32,128]{2,1,0:T(8,128)S(1)}, f32[4,32,128]{2,1,0:T(8,128)S(1)}, f32[4,32,128]{2,1,0:T(8,128)S(1)}, f32[4,32,128]{2,1,0:T(8,1...) while((s32[]{:T(128)}, f32[4,32,128]{2,1,0:T(8,128)S(1)}, ...), condition=%wide.region_40.41_spmd, body=%wide.region_37.40_spmd.sunk | while | flops 409125 | bytes 2921564 | solution.py:112
  (1707 shorter events, 330.9 us)
Async XLA Ops:
  6.5 92.6 %all-gather.22.cloned.1.call-start = ((), (), s32[]{:S(2)}) async-start(), calls=%async_computation | async-start | bytes 2162688 | tf_op jit(solution)/shard_map/all_gather | solution.py:96
  7.4 357.5 %all-gather.24.cloned.1.call-start = ((), (), s32[]{:S(2)}) async-start(), calls=%async_computation.1 | async-start | bytes 2162688 | tf_op jit(solution)/shard_map/all_gather | solution.py:102
  170.5 6.2 copy-start.5
  170.5 18.2 %copy-start = (f32[4,32,128]{2,1,0:T(8,128)S(1)}, f32[4,32,128]{2,1,0:T(8,128)}, u32[]{:S(2)}) copy-start(f32[4,32,128]{2,1,0:T(8,128)} %get-tuple-element.2573) | copy-start | bytes 196612
  170.5 18.2 %copy-start.2 = (f32[1,4,32,128]{3,2,1,0:T(8,128)S(1)}, f32[1,4,32,128]{3,2,1,0:T(8,128)}, u32[]{:S(2)}) copy-start(f32[1,4,32,128]{3,2,1,0:T(8,128)} %param.46) | copy-start | bytes 196612
  170.5 18.2 %copy-start.4 = (f32[4,32,128]{2,1,0:T(8,128)S(1)}, f32[4,32,128]{2,1,0:T(8,128)}, u32[]{:S(2)}) copy-start(f32[4,32,128]{2,1,0:T(8,128)} %param.45) | copy-start | bytes 196612
  208.2 12.1 %copy-start.1 = (f32[4,32,128]{2,1,0:T(8,128)S(1)}, f32[4,32,128]{2,1,0:T(8,128)}, u32[]{:S(2)}) copy-start(f32[4,32,128]{2,1,0:T(8,128)} %get-tuple-element.2579) | copy-start | bytes 196612
  285.5 362.8 %all-gather.26.cloned.1.call-start = ((), (), s32[]{:S(2)}) async-start(), calls=%async_computation.2 | async-start | bytes 2162688 | tf_op jit(solution)/shard_map/all_gather | solution.py:102
  725.8 0.6 copy-start.3
Sparse Core Ops, SparseCore 0:
  10.5 88.6 all-gather.21
  285.7 79.2 all-gather.23
  569.1 79.2 all-gather.25
where the time goes:
time: 741 us; the launch traced here: 733 us
  other arithmetic  264 us (36%)
  waiting for transfers between devices  247 us (33%)
  blocking collectives  124 us (17%)
  local copies, waits for them, and re-layouts  73.4 us (10%)
  between operations  14.4 us (2%)
  loops' own time  10.6 us (1%)
    all_gather x2, waiting for transfers between devices, chain(): all_corrections = lax.all_gather(correction[None], 'tm', axis=0, tiled=True)  159 us
    all_gather x8, blocking collectives, couple(): gathered = lax.all_gather(exported, 'frac', axis=0, tiled=True)  124 us
    all_gather x1, waiting for transfers between devices, body(): all_sources = lax.all_gather(sources, 'tm', axis=0, tiled=True)  88 us
    add x94, other arithmetic, implicit(): right_side = storage_rate * pressure + slice_source  82.8 us
    select_n x93, other arithmetic, turn(): kept_state = jnp.where(slice_index == turn_index + 1, current, kept_state)  55 us
    gather x8, local copies, waits for them, and re-layouts, couple(): remote_values = gathered[trace_source]  49.2 us
    scatter-add x8, other arithmetic, couple(): return jnp.zeros_like(flat_field).at[inter_local].add(weights * remote_va...  47.6 us
    div x254, other arithmetic, sweep(): return (right_side + beside) / diagonal_total  25 us
  transfers between devices with their start and end apart: 3, of which 3 were waited for; matrix products, arithmetic and copies ran while one was open for 0% of the time, Pallas kernels for 0%

commit v1 on v0

--- a/solution.py
+++ b/solution.py
@@ -99,7 +99,9 @@
         if carry_zero:
             all_corrections = jnp.zeros_like(all_sources)
         else:
-            all_corrections = lax.all_gather(correction[None], "tm", axis=0, tiled=True)
+            block = correction[None]
+            sent = jnp.stack([block] * lax.axis_size("tm"))
+            all_corrections = jnp.concatenate(lax.all_to_all(sent, "tm", 0, 0), axis=0)
 
         def turn(turn_index, carried):
             current, kept_state = carried

time: 741 us -> 640 us (0.86)
  the two profiles are of different devices: /device:TPU:8 before, /device:TPU:5 now
where the time goes in v1:
time: 640 us; the launch traced here: 635 us
  other arithmetic  210 us (33%)
  waiting for transfers between devices  182 us (28%)
  blocking collectives  128 us (20%)
  local copies, waits for them, and re-layouts  76.7 us (12%)
  between operations  14.7 us (2%)
  starting transfers between devices  12.3 us (2%)
  loops' own time  10.8 us (2%)
    all_gather x8, blocking collectives, couple(): gathered = lax.all_gather(exported, 'frac', axis=0, tiled=True)  128 us
    all_to_all x2, waiting for transfers between devices, chain(): all_corrections = jnp.concatenate(lax.all_to_all(sent, 'tm', 0, 0), axis=0)  99.9 us
    add x94, other arithmetic, implicit(): right_side = storage_rate * pressure + slice_source  82.8 us
    all_gather x1, waiting for transfers between devices, body(): all_sources = lax.all_gather(sources, 'tm', axis=0, tiled=True)  82.3 us
    gather x8, local copies, waits for them, and re-layouts, couple(): remote_values = gathered[trace_source]  49.2 us
    scatter-add x8, other arithmetic, couple(): return jnp.zeros_like(flat_field).at[inter_local].add(weights * remote_va...  47.6 us
    div x254, other arithmetic, sweep(): return (right_side + beside) / diagonal_total  25 us
    slice x254, other arithmetic, next_cols(): array[:, :, 1:]  20.6 us
  transfers between devices with their start and end apart: 3, of which 3 were waited for; matrix products, arithmetic and copies ran while one was open for 0% of the time, Pallas kernels for 0%

profile of v1, /device:TPU:5, one launch (start us, length us, event | category | flops | bytes accessed | tf_op | source)
XLA Modules:
  0.0 634.8 jit_solution(13973755785336166617)
XLA Ops:
  11.1 82.3 %all-gather.18.cloned.1.call-done = f32[32,4,32,128]{3,2,1,0:T(8,128)} async-done(((f32[1,4,32,128]{3,2,1,0:T(8,128)}), f32[32,4,32,128]{3,2,1,0:T(8,128)}) %all-gather.18.cloned.1.call-update) | async-done | bytes 2097168 | tf_op jit(solution)/shard_map/all_gather | solution.py:96
  93.4 52.9 %while.235 = (s32[]{:T(128)}, f32[4,32,128]{2,1,0:T(8,128)S(1)}, f32[4,32,128]{2,1,0:T(8,128)S(1)}, f32[4,32,128]{2,1,0:T(8,128)}, f32[4,32,128]{2,1,0:T(8,128)}...) while((s32[]{:T(128)}, f32[4,32,128]{2,1,0:T(8,128)S(1)}, ...), condition=%wide.region_3.4_spmd, body=%wide.region_0.3_spmd.sunk | while | flops 392741 | bytes 2790472 | solution.py:114
  149.0 21.9 %all-gather.8 = f32[16,1,256]{2,1,0:T(1,128)S(1)} all-gather(f32[1,1,256]{2,1,0:T(1,128)S(1)} %bitcast.174), channel_id=2, replica_groups=mesh['tm'=32,'frac'=16] {'frac'}, dimensions={0}, use_global_device_ids=true | all-gather | bytes 17408 | tf_op jit(solution)/shard_map/all_gather | solution.py:84
  170.9 6.2 gather_fusion.1
  192.7 15.2 %all-gather.9 = f32[16,1,256]{2,1,0:T(1,128)S(1)} all-gather(f32[1,1,256]{2,1,0:T(1,128)S(1)} %bitcast.175), channel_id=3, replica_groups=mesh['tm'=32,'frac'=16] {'frac'}, dimensions={0}, use_global_device_ids=true | all-gather | bytes 17408 | tf_op jit(solution)/shard_map/all_gather | solution.py:84
  207.9 6.1 gather_fusion.3
  223.8 15.1 %all-gather.10 = f32[16,1,256]{2,1,0:T(1,128)S(1)} all-gather(f32[1,1,256]{2,1,0:T(1,128)S(1)} %bitcast.176), channel_id=4, replica_groups=mesh['tm'=32,'frac'=16] {'frac'}, dimensions={0}, use_global_device_ids=true | all-gather | bytes 17408 | tf_op jit(solution)/shard_map/all_gather | solution.py:84
  238.9 6.1 gather_fusion.5
  245.0 5.9 scatter_custom_fusion.3
  254.8 15.2 %all-gather.11 = f32[16,1,256]{2,1,0:T(1,128)S(1)} all-gather(f32[1,1,256]{2,1,0:T(1,128)S(1)} %bitcast.177), channel_id=5, replica_groups=mesh['tm'=32,'frac'=16] {'frac'}, dimensions={0}, use_global_device_ids=true | all-gather | bytes 17408 | tf_op jit(solution)/shard_map/all_gather | solution.py:84
  270.0 6.1 gather_fusion.7
  286.2 6.6 %all-to-all-start = ((f32[32,1,4,32,128]{4,3,2,1,0:T(8,128)}), f32[32,1,4,32,128]{4,3,2,1,0:T(8,128)S(1)}, u32[]{:S(2)}, u32[]{:S(2)}) async-start(f32[32,1,4,32,128]{4,3,2,1,0:T(8,128)} %stack.6), calls=%async_computation | async-start | bytes 4194304 | tf_op jit(solution)/shard_map/all_to_all | solution.py:104
  292.8 49.9 %all-to-all-done = f32[32,1,4,32,128]{4,3,2,1,0:T(8,128)S(1)} async-done(((f32[32,1,4,32,128]{4,3,2,1,0:T(8,128)}), f32[32,1,4,32,128]{4,3,2,1,0:T(8,128)S(1)}, u32[]{:S(2)}, u32[]{:S(2)}) %all-to-all-start) | async-done | bytes 2097184 | tf_op jit(solution)/shard_map/all_to_all | solution.py:104
  342.7 51.1 %while.242 = (s32[]{:T(128)}, f32[4,32,128]{2,1,0:T(8,128)S(1)}, f32[4,32,128]{2,1,0:T(8,128)S(1)}, f32[4,32,128]{2,1,0:T(8,128)S(1)}, f32[4,32,128]{2,1,0:T(8,1...) while((s32[]{:T(128)}, f32[4,32,128]{2,1,0:T(8,128)S(1)}, ...), condition=%wide.region_22.23_spmd, body=%wide.region_19.22_spmd.sunk | while | flops 409125 | bytes 2921564 | solution.py:114
  395.6 15.4 %all-gather.12 = f32[16,1,256]{2,1,0:T(1,128)S(1)} all-gather(f32[1,1,256]{2,1,0:T(1,128)S(1)} %bitcast.178), channel_id=6, replica_groups=mesh['tm'=32,'frac'=16] {'frac'}, dimensions={0}, use_global_device_ids=true | all-gather | bytes 17408 | tf_op jit(solution)/shard_map/all_gather | solution.py:84
  411.1 6.1 gather_fusion.9
  426.9 15.2 %all-gather.13 = f32[16,1,256]{2,1,0:T(1,128)S(1)} all-gather(f32[1,1,256]{2,1,0:T(1,128)S(1)} %bitcast.179), channel_id=7, replica_groups=mesh['tm'=32,'frac'=16] {'frac'}, dimensions={0}, use_global_device_ids=true | all-gather | bytes 17408 | tf_op jit(solution)/shard_map/all_gather | solution.py:84
  442.2 6.1 gather_fusion.11
  458.1 15.1 %all-gather.14 = f32[16,1,256]{2,1,0:T(1,128)S(1)} all-gather(f32[1,1,256]{2,1,0:T(1,128)S(1)} %bitcast.180), channel_id=8, replica_groups=mesh['tm'=32,'frac'=16] {'frac'}, dimensions={0}, use_global_device_ids=true | all-gather | bytes 17408 | tf_op jit(solution)/shard_map/all_gather | solution.py:84
  473.2 6.1 gather_fusion.13
  489.0 15.2 %all-gather.15 = f32[16,1,256]{2,1,0:T(1,128)S(1)} all-gather(f32[1,1,256]{2,1,0:T(1,128)S(1)} %bitcast.173), channel_id=9, replica_groups=mesh['tm'=32,'frac'=16] {'frac'}, dimensions={0}, use_global_device_ids=true | all-gather | bytes 17408 | tf_op jit(solution)/shard_map/all_gather | solution.py:84
  504.3 6.1 gather_fusion.15
  526.2 49.9 %all-to-all-done.1 = f32[32,1,4,32,128]{4,3,2,1,0:T(8,128)S(1)} async-done(((f32[32,1,4,32,128]{4,3,2,1,0:T(8,128)}), f32[32,1,4,32,128]{4,3,2,1,0:T(8,128)S(1)}, u32[]{:S(2)}, u32[]{:S(2)}) %all-to-all-start.1) | async-done | bytes 2097184 | tf_op jit(solution)/shard_map/all_to_all | solution.py:104
  576.2 51.1 %while.249 = (s32[]{:T(128)}, f32[4,32,128]{2,1,0:T(8,128)S(1)}, f32[4,32,128]{2,1,0:T(8,128)S(1)}, f32[4,32,128]{2,1,0:T(8,128)S(1)}, f32[4,32,128]{2,1,0:T(8,1...) while((s32[]{:T(128)}, f32[4,32,128]{2,1,0:T(8,128)S(1)}, ...), condition=%wide.region_40.41_spmd, body=%wide.region_37.40_spmd.sunk | while | flops 409125 | bytes 2921564 | solution.py:114
  (1707 shorter events, 291.4 us)
Async XLA Ops:
  6.5 86.8 %all-gather.18.cloned.1.call-start = ((), (), s32[]{:S(2)}) async-start(), calls=%async_computation.2 | async-start | bytes 2162688 | tf_op jit(solution)/shard_map/all_gather | solution.py:96
  170.9 6.2 copy-start.5
  170.9 18.2 %copy-start = (f32[4,32,128]{2,1,0:T(8,128)S(1)}, f32[4,32,128]{2,1,0:T(8,128)}, u32[]{:S(2)}) copy-start(f32[4,32,128]{2,1,0:T(8,128)} %get-tuple-element.2571) | copy-start | bytes 196612
  170.9 18.2 %copy-start.2 = (f32[1,4,32,128]{3,2,1,0:T(8,128)S(1)}, f32[1,4,32,128]{3,2,1,0:T(8,128)}, u32[]{:S(2)}) copy-start(f32[1,4,32,128]{3,2,1,0:T(8,128)} %param.46) | copy-start | bytes 196612
  170.9 18.2 %copy-start.4 = (f32[4,32,128]{2,1,0:T(8,128)S(1)}, f32[4,32,128]{2,1,0:T(8,128)}, u32[]{:S(2)}) copy-start(f32[4,32,128]{2,1,0:T(8,128)} %param.45) | copy-start | bytes 196612
  207.9 12.1 %copy-start.1 = (f32[4,32,128]{2,1,0:T(8,128)S(1)}, f32[4,32,128]{2,1,0:T(8,128)}, u32[]{:S(2)}) copy-start(f32[4,32,128]{2,1,0:T(8,128)} %get-tuple-element.2577) | copy-start | bytes 196612
  286.2 56.5 %all-to-all-start = ((f32[32,1,4,32,128]{4,3,2,1,0:T(8,128)}), f32[32,1,4,32,128]{4,3,2,1,0:T(8,128)S(1)}, u32[]{:S(2)}, u32[]{:S(2)}) async-start(f32[32,1,4,32,128]{4,3,2,1,0:T(8,128)} %stack.6), calls=%async_computation | async-start | bytes 4194304 | tf_op jit(solution)/shard_map/all_to_all | solution.py:104
  520.5 55.7 %all-to-all-start.1 = ((f32[32,1,4,32,128]{4,3,2,1,0:T(8,128)}), f32[32,1,4,32,128]{4,3,2,1,0:T(8,128)S(1)}, u32[]{:S(2)}, u32[]{:S(2)}) async-start(f32[32,1,4,32,128]{4,3,2,1,0:T(8,128)} %stack.7), calls=%async_computation.1 | async-start | bytes 4194304 | tf_op jit(solution)/shard_map/all_to_all | solution.py:104
  627.3 0.6 copy-start.3
Sparse Core Ops, SparseCore 0:
  10.5 82.8 all-gather.17
